TPU v7x, 32 devices: a whole 2x2x4 slice. The times are simulated.
32 devices in a mesh: row: 4 (over y, core), col: 8 (over z, x).
Axes of the slice: x: 2, y: 2, z: 4, core: 2. Of those that a mesh axis runs over, the one named last changes fastest.
Arguments:
- positions: float32 [3, 16384], P(None, ('row', 'col')), may hold values from 0 to 4
- momenta: float32 [3, 16384], P(None, ('row', 'col')), may hold values from -6 to 6
- species: int32 [16384], P(('row', 'col')), may hold values from 0 to 1
- tile_a: int32 [4, 8, 256], P('row', 'col'), may hold values from 0 to 31, as said below
- tile_b: int32 [4, 8, 256], P('row', 'col'), may hold values from 0 to 15
- tile_count: int32 [4, 8], P('row', 'col'), may hold values from 1 to 256, as said below
Outputs:
- trial_positions: float32 [3, 16384], P(None, ('row', 'col'))
- trial_momenta: float32 [3, 16384], P(None, ('row', 'col'))
- end_force: float32 [3, 16384], P(None, ('row', 'col'))
Inputs may be any that keep to these rules, and one draw needn't show every extreme that they name: Live slots of one grid cell name distinct (tile_a, tile_b) pairs; slots from tile_count on hold 0. `tile_count`: some grid cell of row 0 has exactly 256 live slots.
All inputs are finite; a program needn't handle non-finite values.
Results may differ from a plain program's by a relative error of at most 0.0003.
Values sent between devices are 32-bit elements; how exact they have to be, the bound alone decides.
A program may use at most 64 MiB of HBM per device.

v0:
```python
import jax
import jax.numpy as jnp
from jax import lax
from jax.sharding import PartitionSpec as P

SCREENING = 1.0
SOFTENING = 0.25
GRAVITY = 0.5
LIGHT_CHARGE = 1.0
HEAVY_CHARGE = 2.5
HALF_STEP = 0.1
TIME_STEP = 0.2
tile_width = 128
block_pairs = 32


def tile_pair_force(near, far, same):
    offset = near[:3, :, :, None] - far[:3, :, None, :]
    radius = jnp.sqrt(jnp.sum(offset * offset, axis=0) + SOFTENING)
    weight = (
        near[3][:, :, None]
        * far[3][:, None, :]
        * jnp.exp(-SCREENING * radius)
        * (1.0 + SCREENING * radius)
        / (radius * radius * radius)
    )
    diagonal = jnp.arange(tile_width)[:, None] == jnp.arange(tile_width)[None, :]
    weight = jnp.where(jnp.logical_and(same[:, None, None], diagonal[None]), 0.0, weight)
    return jnp.transpose(jnp.sum(weight[None] * offset, axis=3), (1, 0, 2))


def weight_of(mass):
    return jnp.zeros((3, mass.shape[0]), jnp.float32).at[2].set(-GRAVITY * mass)


def pair_forces(
    row_state, column_state, firsts, seconds, count, row_index, col_index, tile_dev, col_count
):
    row_tiles = row_state.reshape(4, -1, tile_width)
    column_tiles = column_state.reshape(4, -1, tile_width)

    def visit(step, total):
        start = step * block_pairs
        first = lax.dynamic_slice_in_dim(firsts, start, block_pairs)
        second = lax.dynamic_slice_in_dim(seconds, start, block_pairs)
        alive = start + jnp.arange(block_pairs, dtype=jnp.int32) < count
        near_id = row_index * col_count * tile_dev + first
        far_id = (second // tile_dev * col_count + col_index) * tile_dev + second % tile_dev
        term = tile_pair_force(row_tiles[:, first], column_tiles[:, second], near_id == far_id)
        term = term * alive.astype(jnp.float32)[:, None, None]
        return total.at[first].add(term)

    rounds = (count + block_pairs - 1) // block_pairs
    empty = jnp.zeros((row_tiles.shape[1], 3, tile_width), jnp.float32)
    total = lax.fori_loop(0, rounds, visit, empty)
    return jnp.transpose(total, (1, 0, 2)).reshape(3, -1)


def per_device(positions, momenta, species, tile_a, tile_b, tile_count):
    own = positions.shape[1]
    tile_dev = own // tile_width
    col_count = lax.axis_size("col")
    row_index = lax.axis_index("row")
    col_index = lax.axis_index("col")
    charge = jnp.where(species == 1, HEAVY_CHARGE, LIGHT_CHARGE).astype(jnp.float32)
    firsts = tile_a[0, 0]
    seconds = tile_b[0, 0]
    count = tile_count[0, 0]

    def columns(state):
        return lax.all_gather(state, "row", axis=1, tiled=True)

    def forces(row_state, column_state):
        return pair_forces(
            row_state,
            column_state,
            firsts,
            seconds,
            count,
            row_index,
            col_index,
            tile_dev,
            col_count,
        )

    packed = jnp.concatenate([positions, charge[None]], axis=0)
    row_state, row_momenta = (
        lax.all_gather(packed, "col", axis=1, tiled=True),
        lax.all_gather(momenta, "col", axis=1, tiled=True),
    )
    whole_force = lax.psum(forces(row_state, columns(packed)), "col") + weight_of(row_state[3])
    row_half = row_momenta + HALF_STEP * whole_force
    row_moved = row_state[:3] + TIME_STEP * row_half / row_state[3]
    offset = col_index * own
    half = lax.dynamic_slice_in_dim(row_half, offset, own, 1)
    moved = lax.dynamic_slice_in_dim(row_moved, offset, own, 1)
    moved_rows = jnp.concatenate([row_moved, row_state[3:4]], axis=0)
    partial_force = forces(moved_rows, columns(jnp.concatenate([moved, charge[None]], axis=0)))
    end_force = lax.psum_scatter(partial_force, "col", scatter_dimension=1, tiled=True) + weight_of(
        charge
    )
    ahead = half + HALF_STEP * end_force
    return (moved, ahead, end_force)


def solution(mesh):
    in_specs = (
        P(None, ("row", "col")),
        P(None, ("row", "col")),
        P(("row", "col")),
        P("row", "col", None),
        P("row", "col", None),
        P("row", "col"),
    )
    out_specs = (P(None, ("row", "col")), P(None, ("row", "col")), P(None, ("row", "col")))
    return jax.shard_map(
        per_device, mesh=mesh, in_specs=in_specs, out_specs=out_specs, check_vma=False
    )
```

profile of v0, /device:TPU:0, one launch (start us, length us, event | category | flops | bytes accessed | tf_op | source)
XLA Modules:
  0.0 396.1 jit_solution(825792002220034260)
XLA Ops:
  9.3 6.2 %all_gather.14 = f32[4,2048]{1,0:T(4,128)S(1)} all-gather(f32[4,512]{1,0:T(4,128)S(1)} %pad_maximum_fusion.1), channel_id=1, replica_groups=mesh['row'=4,'col'=8] {'row'}, dimensions={1}, use_global_device_ids=true | all-gather | bytes 40960 | tf_op jit(solution)/shard_map/all_gather | solution.py:71
  15.4 31.3 %all_gather.12 = f32[4,4096]{1,0:T(4,128)S(1)} all-gather(f32[4,512]{1,0:T(4,128)S(1)} %pad_maximum_fusion.1), channel_id=1, replica_groups=mesh['row'=4,'col'=8] {'col'}, dimensions={1}, use_global_device_ids=true | all-gather | bytes 73728 | tf_op jit(solution)/shard_map/all_gather | solution.py:88
  46.7 30.7 %all_gather.13 = f32[3,4096]{1,0:T(4,128)S(1)} all-gather(f32[3,512]{1,0:T(4,128)} %param.15), channel_id=1, replica_groups=mesh['row'=4,'col'=8] {'col'}, dimensions={1}, use_global_device_ids=true | all-gather | bytes 55296 | tf_op jit(solution)/shard_map/all_gather | solution.py:89
  77.4 65.9 %while.26 = (s32[]{:T(128)}, f32[32,3,128]{2,1,0:T(4,128)S(1)}, s32[]{:T(128)}, s32[256]{0:T(256)}, s32[]{:T(128)}, /*index=5*/s32[256]{0:T(256)}, s32[]{:T(128)...) while((s32[]{:T(128)}, f32[32,3,128]{2,1,0:T(4,128)S(1)}, ...), condition=%wide.region_4.5_spmd, body=%wide.region_0.4_spmd.sunk | while | flops 14711878 | bytes 9578379 | solution.py:55
  77.4 1.4 compare_convert_fusion.4
  81.0 2.1 fusion.18
  83.1 1.9 fusion.19
  85.0 3.8 fusion.20
  88.9 1.7 scatter_fusion
  90.6 1.4 compare_convert_fusion.4
  92.0 0.8 compare_select_fusion.13
  94.2 2.1 fusion.18
  96.2 1.9 fusion.19
  98.1 3.8 fusion.20
  102.1 1.7 scatter_fusion
  103.8 1.4 compare_convert_fusion.4
  107.3 2.1 fusion.18
  109.4 1.9 fusion.19
  111.3 3.8 fusion.20
  115.3 1.6 scatter_fusion
  116.9 1.4 compare_convert_fusion.4
  118.4 0.8 compare_select_fusion.13
  120.5 2.1 fusion.18
  122.6 1.9 fusion.19
  124.5 3.8 fusion.20
  128.4 1.7 scatter_fusion
  130.1 1.4 compare_convert_fusion.4
  131.5 0.8 compare_select_fusion.13
  133.6 2.1 fusion.18
  135.7 1.9 fusion.19
  137.6 3.8 fusion.20
  141.6 1.7 scatter_fusion
  143.3 68.3 %psum.9 = f32[3,4096]{1,0:T(4,128)S(1)} all-reduce(f32[3,4096]{1,0:T(4,128)S(1)} %bitcast.79), channel_id=1, replica_groups=mesh['row'=4,'col'=8] {'col'}, use_global_device_ids=true, to_apply=%region_5.6 | all-reduce | flops 12288 | bytes 98304 | tf_op jit(solution)/shard_map/psum | solution.py:91
  212.0 5.2 %all_gather.15 = f32[4,2048]{1,0:T(4,128)S(1)} all-gather(f32[4,512]{1,0:T(4,128)S(1)} %pad_maximum_fusion), channel_id=1, replica_groups=mesh['row'=4,'col'=8] {'row'}, dimensions={1}, use_global_device_ids=true | all-gather | bytes 40960 | tf_op jit(solution)/shard_map/all_gather | solution.py:71
  217.3 65.9 %while.27 = (s32[]{:T(128)}, f32[32,3,128]{2,1,0:T(4,128)S(1)}, s32[]{:T(128)}, s32[256]{0:T(256)}, s32[]{:T(128)}, /*index=5*/s32[256]{0:T(256)}, s32[]{:T(128)...) while((s32[]{:T(128)}, f32[32,3,128]{2,1,0:T(4,128)S(1)}, ...), condition=%wide.region_10.11_spmd, body=%wide.region_6.10_spmd.sunk | while | flops 14711878 | bytes 9578379 | solution.py:55
  217.3 1.4 compare_convert_fusion.5
  218.7 0.8 compare_select_fusion.14
  220.8 2.1 fusion.21
  222.9 1.9 fusion.22
  224.8 3.8 fusion.23
  228.8 1.7 scatter_fusion.1
  230.4 1.4 compare_convert_fusion.5
  234.0 2.1 fusion.21
  236.1 1.9 fusion.22
  238.0 3.8 fusion.23
  241.9 1.7 scatter_fusion.1
  243.6 1.4 compare_convert_fusion.5
  247.2 2.1 fusion.21
  249.2 1.9 fusion.22
  251.1 3.8 fusion.23
  255.1 1.6 scatter_fusion.1
  256.8 1.4 compare_convert_fusion.5
  260.3 2.1 fusion.21
  262.4 1.9 fusion.22
  264.3 3.8 fusion.23
  268.2 1.7 scatter_fusion.1
  269.9 1.4 compare_convert_fusion.5
  273.5 2.1 fusion.21
  275.6 1.9 fusion.22
  277.4 3.8 fusion.23
  281.4 1.7 scatter_fusion.1
  283.1 2.0 copy.43
  285.2 102.3 %reduce-scatter.4.cloned.1.call-done = f32[512,3]{1,0:T(8,128)} async-done(((f32[4096,3]{1,0:T(8,128)}), f32[512,3]{1,0:T(8,128)}) %reduce-scatter.4.cloned.1.call-update) | async-done | bytes 6160
  387.5 1.1 copy.44
  (135 shorter events, 21.3 us)
Async XLA Ops:
  7.2 380.3 %reduce-scatter.4.cloned.1.call-start = ((), (), s32[]{:S(2)}) async-start(), calls=%async_computation.1 | async-start | bytes 2359296
  212.0 5.2 %copy-start.1 = (f32[3,512]{1,0:T(4,128)}, f32[3,512]{1,0:T(4,128)S(1)}, u32[]{:S(2)}) copy-start(f32[3,512]{1,0:T(4,128)S(1)} %constant_dynamic-slice_fusion) | copy-start | bytes 18436
  388.6 0.6 copy-start
Sparse Core Ops, SparseCore 0:
  285.3 102.1 reduce-scatter.3
where the time goes:
time: 402 us; the launch traced here: 396 us
  blocking collectives  142 us (35%)
  other arithmetic  120 us (30%)
  waiting for transfers between devices  102 us (25%)
  local copies, waits for them, and re-layouts  16.4 us (4%)
  between operations  14.8 us (4%)
    unnamed x2, waiting for transfers between devices  102 us
    psum x1, blocking collectives, per_device(): lax.psum(forces(row_state, columns(packed)), 'col')  68.3 us
    reduce_sum x10, other arithmetic, tile_pair_force(): return jnp.transpose(jnp.sum(weight[None] * offset, axis=3), (1, 0, 2))  38.3 us
    all_gather x1, blocking collectives, per_device(): lax.all_gather(packed, 'col', axis=1, tiled=True)  31.3 us
    all_gather x1, blocking collectives, per_device(): lax.all_gather(momenta, 'col', axis=1, tiled=True)  30.7 us
    reduce_sum x10, other arithmetic, tile_pair_force(): radius = jnp.sqrt(jnp.sum(offset * offset, axis=0) + SOFTENING)  20.7 us
    select_n x10, other arithmetic, tile_pair_force(): jnp.where(jnp.logical_and(same[:, None, None], diagonal[None]), 0.0, weight)  18.8 us
    scatter-add x10, other arithmetic, visit(): return total.at[first].add(term)  16.6 us
  transfers between devices with their start and end apart: 1, of which 1 were waited for; matrix products, arithmetic and copies ran while one was open for 0% of the time, Pallas kernels for 0%

commit v1 on v0

v1 whole, which is shorter than its diff:
```python
import functools
import math

import jax
import jax.numpy as jnp
from jax import lax
from jax.experimental import pallas as pl
from jax.experimental.pallas import tpu as pltpu
from jax.sharding import PartitionSpec as P

SOFTENING = 0.25
GRAVITY = 0.5
LIGHT_CHARGE = 1.0
HEAVY_CHARGE = 2.5
HALF_STEP = 0.1
TIME_STEP = 0.2
tile_width = 128
unroll = 4
scale = 1.0 / math.log(2.0)
middle = 2.0
depth = 32
MESH = pl.DeviceIdType.MESH


def peers_of(axes):
    found = []
    for axis, size in axes:
        me = lax.axis_index(axis)
        for step in range(1, size):
            found.append((axis, lax.rem(me + step, size)))
    return found


def greet(axes):
    barrier = pltpu.get_barrier_semaphore()
    everyone = peers_of(axes)
    for axis, peer in everyone:
        pl.semaphore_signal(barrier, inc=1, device_id={axis: peer}, device_id_type=MESH)
    pl.semaphore_wait(barrier, len(everyone))


def charge_of(species):
    return jnp.where(species == 1, HEAVY_CHARGE, LIGHT_CHARGE).astype(jnp.float32)


def spread(axes, packed, slots, send_sem, recv_sem):
    copies = []
    for (axis, size), buffer in zip(axes, slots):
        me = lax.axis_index(axis)
        for step in range(1, size):
            which = len(copies)
            copies.append(
                pltpu.make_async_remote_copy(
                    src_ref=packed,
                    dst_ref=buffer.at[me],
                    send_sem=send_sem.at[which],
                    recv_sem=recv_sem.at[which],
                    device_id={axis: lax.rem(me + step, size)},
                    device_id_type=MESH,
                )
            )
    for copy in copies:
        copy.start()
    for (axis, size), buffer in zip(axes, slots):
        buffer[pl.ds(lax.axis_index(axis), 1)] = packed[...][None]
    for copy in copies:
        copy.wait()


def pack(packed, places, charge, tiles):
    for tile in range(tiles):
        lanes = slice(tile * tile_width, (tile + 1) * tile_width)
        packed[4 * tile : 4 * tile + 3, :] = places[:, lanes]
        packed[4 * tile + 3 : 4 * tile + 4, :] = charge[:, lanes]


def gather_kernel(axes, tiles, pos_ref, spec_ref, rows_ref, cols_ref, packed, send_sem, recv_sem):
    greet(axes)
    pack(packed, pos_ref[...], charge_of(spec_ref[...]), tiles)
    spread(axes, packed, (rows_ref, cols_ref), send_sem, recv_sem)


def collect(axis, size, partial, arrived, send_sem, recv_sem):
    me = lax.axis_index(axis)
    copies = []
    for step in range(1, size):
        peer = lax.rem(me + step, size)
        copies.append(
            pltpu.make_async_remote_copy(
                src_ref=partial.at[peer],
                dst_ref=arrived.at[me],
                send_sem=send_sem.at[step - 1],
                recv_sem=recv_sem.at[step - 1],
                device_id={axis: peer},
                device_id_type=MESH,
            )
        )
    for copy in copies:
        copy.start()
    arrived[pl.ds(me, 1)] = partial[pl.ds(me, 1)]
    for copy in copies:
        copy.wait()
    total = arrived[0]
    for index in range(1, size):
        total = total + arrived[index]
    return total


def unpacked(total, charge, tiles):
    force = jnp.concatenate([total[4 * tile : 4 * tile + 3, :] for tile in range(tiles)], axis=1)
    third = lax.broadcasted_iota(jnp.int32, force.shape, 0) == 2
    return force + jnp.where(third, -GRAVITY * charge, 0.0)


def step_kernel(
    axes, tiles, part_ref, pos_ref, mom_ref, spec_ref, rows_ref, cols_ref, moved_ref, half_ref,
    arrived, packed, send_a, recv_a, send_b, recv_b,
):
    greet(axes)
    charge = charge_of(spec_ref[...])
    total = collect(axes[0][0], axes[0][1], part_ref, arrived, send_a, recv_a)
    force = unpacked(total, charge, tiles)
    half = mom_ref[...] + HALF_STEP * force
    moved = pos_ref[...] + TIME_STEP * half / charge
    half_ref[...] = half
    moved_ref[...] = moved
    pack(packed, moved, charge, tiles)
    spread(axes, packed, (rows_ref, cols_ref), send_b, recv_b)


def last_kernel(axes, tiles, part_ref, half_ref, spec_ref, ahead_ref, force_ref, arrived, send_a, recv_a):
    greet(axes)
    charge = charge_of(spec_ref[...])
    total = collect(axes[0][0], axes[0][1], part_ref, arrived, send_a, recv_a)
    force = unpacked(total, charge, tiles)
    force_ref[...] = force
    ahead_ref[...] = half_ref[...] + HALF_STEP * force


def pieces(value):
    high = value.astype(jnp.bfloat16).astype(jnp.float32)
    rest = value - high
    mid = rest.astype(jnp.bfloat16).astype(jnp.float32)
    return high, mid, (rest - mid).astype(jnp.bfloat16).astype(jnp.float32)


pairs_of_pieces = ((0, 0), (0, 1), (1, 0), (0, 2), (2, 0), (1, 1))


def force_kernel(
    tiles, first_ref, second_ref, count_ref, rows_ref, cols_ref, out_ref,
    near_f, near, far_f, far, load_f, load, total,
):
    near_f[...] = jnp.zeros_like(near_f)
    far_f[...] = jnp.zeros_like(far_f)
    load_f[...] = jnp.zeros_like(load_f)
    total[...] = jnp.zeros_like(total)

    def component(ref, owner, index):
        return ref[owner, pl.ds(index, tiles, stride=4), :]

    for owner in range(rows_ref.shape[0]):
        here = pl.ds(owner * tiles, tiles)
        square = 0.0
        for axis in range(3):
            value = (component(rows_ref, owner, axis) - middle) * scale
            square = square + value * value
            split = pieces(value)
            for row, (left, _) in enumerate(pairs_of_pieces):
                near_f[here, 6 * axis + row, :] = -2.0 * split[left]
        for row, piece in enumerate(pieces(square)):
            near_f[here, 18 + row, :] = piece
            near_f[here, 21 + row, :] = jnp.ones_like(piece)
    near[...] = near_f[...].astype(jnp.bfloat16)

    for owner in range(cols_ref.shape[0]):
        here = pl.ds(owner * tiles, tiles)
        charge = component(cols_ref, owner, 3)
        square = SOFTENING * scale * scale
        for axis in range(3):
            value = (component(cols_ref, owner, axis) - middle) * scale
            square = square + value * value
            split = pieces(value)
            for row, (_, right) in enumerate(pairs_of_pieces):
                far_f[here, 6 * axis + row, :] = split[right]
            for row, piece in enumerate(pieces(charge * value)):
                load_f[here, 4 * row + axis, :] = piece
        load_f[here, 3, :] = charge
        for row, piece in enumerate(pieces(square)):
            far_f[here, 18 + row, :] = jnp.ones_like(piece)
            far_f[here, 21 + row, :] = piece
    for tile in range(cols_ref.shape[0] * tiles):
        far[tile] = far_f[tile].T.astype(jnp.bfloat16)
    single = load_f[...].astype(jnp.bfloat16)
    load[:, :, :tile_width] = single
    load[:, :, tile_width:] = single

    count = count_ref[0]

    def visit(step, carry):
        start = step * unroll
        firsts = [first_ref[start + index] for index in range(unroll)]
        seconds = [second_ref[start + index] for index in range(unroll)]
        terms = []
        for index in range(unroll):
            square = jnp.dot(far[seconds[index]], near[firsts[index]], preferred_element_type=jnp.float32)
            square = jnp.maximum(square, SOFTENING * scale * scale)
            inverse = lax.rsqrt(square)
            decay = jnp.exp2(-(square * inverse))
            weight = decay * (inverse * inverse) * (inverse + 1.0 / scale)
            high = weight.astype(jnp.bfloat16)
            low = (weight - high.astype(jnp.float32)).astype(jnp.bfloat16)
            both = jnp.concatenate([high, low], axis=0)
            term = jnp.dot(load[seconds[index]], both, preferred_element_type=jnp.float32)
            terms.append(jnp.where(start + index < count, term, 0.0))
        for index in range(unroll):
            total[firsts[index]] += terms[index]
        return carry

    lax.fori_loop(0, (count + unroll - 1) // unroll, visit, 0)

    for owner in range(rows_ref.shape[0]):
        here = pl.ds(owner * tiles, tiles)
        charge = component(rows_ref, owner, 3) * (scale * scale)
        weights = total[here, 3, :]
        for axis in range(3):
            value = (component(rows_ref, owner, axis) - middle) * scale
            moment = total[here, axis, :] + total[here, 4 + axis, :] + total[here, 8 + axis, :]
            out_ref[owner, pl.ds(axis, tiles, stride=4), :] = charge * (value * weights - moment)
        out_ref[owner, pl.ds(3, tiles, stride=4), :] = jnp.zeros_like(charge)


def per_device(row_count, col_count, positions, momenta, species, tile_a, tile_b, tile_count):
    own = positions.shape[1]
    tiles = own // tile_width
    f32 = jnp.float32
    axes = (("col", col_count), ("row", row_count))
    others = row_count + col_count - 2
    vmem = pl.BlockSpec(memory_space=pltpu.VMEM)
    smem = pl.BlockSpec(memory_space=pltpu.SMEM)
    labels = species.reshape(1, own)
    slots = tile_a.shape[-1]
    padding = -slots % unroll
    firsts = jnp.pad(tile_a.reshape(slots), (0, padding))
    seconds = jnp.pad(tile_b.reshape(slots), (0, padding))
    count = tile_count.reshape(1)
    row_shape = jax.ShapeDtypeStruct((col_count, 4 * tiles, tile_width), f32)
    col_shape = jax.ShapeDtypeStruct((row_count, 4 * tiles, tile_width), f32)
    own_shape = jax.ShapeDtypeStruct((3, own), f32)
    DMA = pltpu.SemaphoreType.DMA

    rows, cols = pl.pallas_call(
        functools.partial(gather_kernel, axes, tiles),
        out_shape=(row_shape, col_shape),
        in_specs=[vmem] * 2,
        out_specs=(vmem, vmem),
        scratch_shapes=[pltpu.VMEM((4 * tiles, tile_width), f32), DMA((others,)), DMA((others,))],
        compiler_params=pltpu.CompilerParams(collective_id=0, has_side_effects=True),
        name="gather",
    )(positions, labels)

    near_count, far_count = col_count * tiles, row_count * tiles
    bf16 = jnp.bfloat16
    forces = pl.pallas_call(
        functools.partial(force_kernel, tiles),
        out_shape=row_shape,
        in_specs=[smem] * 3 + [vmem] * 2,
        out_specs=vmem,
        scratch_shapes=[
            pltpu.VMEM((near_count, depth, tile_width), f32),
            pltpu.VMEM((near_count, depth, tile_width), bf16),
            pltpu.VMEM((far_count, depth, tile_width), f32),
            pltpu.VMEM((far_count, tile_width, depth), bf16),
            pltpu.VMEM((far_count, 16, tile_width), f32),
            pltpu.VMEM((far_count, 16, 2 * tile_width), bf16),
            pltpu.VMEM((near_count, 16, tile_width), f32),
        ],
        compiler_params=pltpu.CompilerParams(vmem_limit_bytes=32 << 20),
        name="forces",
    )

    partial = forces(firsts, seconds, count, rows, cols)
    rows, cols, moved, half = pl.pallas_call(
        functools.partial(step_kernel, axes, tiles),
        out_shape=(row_shape, col_shape, own_shape, own_shape),
        in_specs=[vmem] * 4,
        out_specs=(vmem,) * 4,
        scratch_shapes=[
            pltpu.VMEM(row_shape.shape, f32),
            pltpu.VMEM((4 * tiles, tile_width), f32),
            DMA((col_count - 1,)),
            DMA((col_count - 1,)),
            DMA((others,)),
            DMA((others,)),
        ],
        compiler_params=pltpu.CompilerParams(collective_id=1, has_side_effects=True),
        name="step",
    )(partial, positions, momenta, labels)

    partial = forces(firsts, seconds, count, rows, cols)
    ahead, end_force = pl.pallas_call(
        functools.partial(last_kernel, axes[:1], tiles),
        out_shape=(own_shape, own_shape),
        in_specs=[vmem] * 3,
        out_specs=(vmem,) * 2,
        scratch_shapes=[pltpu.VMEM(row_shape.shape, f32), DMA((col_count - 1,)), DMA((col_count - 1,))],
        compiler_params=pltpu.CompilerParams(collective_id=2, has_side_effects=True),
        name="last",
    )(partial, half, labels)
    return (moved, ahead, end_force)


def solution(mesh):
    in_specs = (
        P(None, ("row", "col")),
        P(None, ("row", "col")),
        P(("row", "col")),
        P("row", "col", None),
        P("row", "col", None),
        P("row", "col"),
    )
    out_specs = (P(None, ("row", "col")), P(None, ("row", "col")), P(None, ("row", "col")))
    body = functools.partial(per_device, mesh.shape["row"], mesh.shape["col"])
    return jax.shard_map(body, mesh=mesh, in_specs=in_specs, out_specs=out_specs, check_vma=False)
```

time: 402 us -> 87.6 us (0.22); the launches traced: 396 us -> 88 us
  blocking collectives: 142 us -> 0 us
  other arithmetic: 120 us -> 0 us
  waiting for transfers between devices: 102 us -> 0 us
  Pallas kernels: 0 us -> 79.5 us
  between operations: 14.8 us -> 1.38 us
  local copies, waits for them, and re-layouts: 16.4 us -> 7.09 us
    unnamed x2 -> x0, waiting for transfers between devices: 102 us -> none
    pallas_call x0 -> x5, Pallas kernels: none -> 79.5 us  [the longest x2 34.8 us: per_device(): partial = forces(firsts, seconds, count, rows, cols)]
    all_gather x4 -> x0, blocking collectives: 73.3 us -> none  [the longest x1 31.3 us: per_device(): lax.all_gather(packed, 'col', axis=1, tiled=True)]
    psum x1 -> x0, blocking collectives: 68.3 us -> none  [per_device(): lax.psum(forces(row_state, columns(packed)), 'col')]
    reduce_sum x20 -> x0, other arithmetic: 59 us -> none  [the longest x10 38.3 us: tile_pair_force(): return jnp.transpose(jnp.sum(weight[None] * offset, axis=3), (1, 0, 2))]
    select_n x20 -> x0, other arithmetic: 26.6 us -> none  [the longest x10 18.8 us: tile_pair_force(): jnp.where(jnp.logical_and(same[:, None, None], diagonal[None]), 0.0, weight)]
    scatter-add x10 -> x0, other arithmetic: 16.6 us -> none  [visit(): return total.at[first].add(term)]
    convert_element_type x10 -> x0, other arithmetic: 14.3 us -> none  [visit(): term = term * alive.astype(jnp.float32)[:, None, None]]
  transfers between devices with their start and end apart: 1 -> 0, of which waited for: 1 -> 0; matrix products, arithmetic and copies ran while one was open for 0% -> 0% of each run, Pallas kernels for 0% -> 0%
where the time goes in v1:
time: 87.6 us; the launch traced here: 88 us
  Pallas kernels  79.5 us (91%)
  local copies, waits for them, and re-layouts  7.09 us (8%)
  between operations  1.38 us (2%)
    pallas_call x2, Pallas kernels, per_device(): partial = forces(firsts, seconds, count, rows, cols)  34.8 us
    pallas_call x1, Pallas kernels, per_device(): pl.pallas_call(functools.partial(step_kernel, axes, tiles), out_shape=(ro...  20.8 us
    pallas_call x1, Pallas kernels, per_device(): pl.pallas_call(functools.partial(last_kernel, axes[:1], tiles), out_shape...  13.2 us
    pallas_call x1, Pallas kernels, per_device(): pl.pallas_call(functools.partial(gather_kernel, axes, tiles), out_shape=(...  10.7 us
    unnamed x25, local copies, waits for them, and re-layouts  7.09 us

profile of v1, /device:TPU:0, one launch (start us, length us, event | category | flops | bytes accessed | tf_op | source)
XLA Modules:
  0.0 88.0 jit_solution(17630717838475202811)
XLA Ops:
  1.3 10.7 %gather.1 = (f32[8,16,128]{2,1,0:T(8,128)}, f32[4,16,128]{2,1,0:T(8,128)}) custom-call(f32[3,512]{1,0:T(4,128)} %pos_ref.3, s32[1,512]{1,0:T(1,128)} %bitcast.10), custom_call_target="tpu_custom_call" | custom-call | tf_op jit(solution)/shard_map/gather/pallas_call | solution.py:252
  12.0 0.0 copy-start.7
  12.0 0.0 copy-start.6
  12.0 0.7 copy-done.7
  12.6 0.0 copy-done.6
  12.7 0.0 copy-start.3
  12.7 0.8 copy-done.3
  13.5 0.0 copy-start.5
  13.5 0.8 copy-done.5
  14.3 17.4 %forces.2.part_ref = f32[8,16,128]{2,1,0:T(8,128)S(1)} custom-call(s32[256]{0:T(256)S(1)} %bitcast.6, s32[256]{0:T(256)S(1)} %bitcast.8, s32[1]{0:T(128)} %bitcast.4.count_ref, f32[8,16,128]{2,1,0:T(8,128)S(1)} %copy-done.3, f32[4,16,128]{2,1,0:T(8,128)S(1)} %copy-done.5), custom_call_target="tpu_custom_call" | custom-call | tf_op jit(solution)/shard_map/forces/pallas_call | solution.py:282
  31.7 0.0 copy-start
  31.7 0.6 copy-done
  32.3 20.8 %step.1 = (f32[8,16,128]{2,1,0:T(8,128)}, f32[4,16,128]{2,1,0:T(8,128)}, f32[3,512]{1,0:T(4,128)}, f32[3,512]{1,0:T(4,128)}) custom-call(f32[8,16,128]{2,1,0:T(8,128)} %copy-done, f32[3,512]{1,0:T(4,128)} %pos_ref.3, f32[3,512]{1,0:T(4,128)} %mom_ref.1, s32[1,512]{1,0:T(1,128)} %bitcast.11), custom_call_target="tpu_custom_call" | custom-call | tf_op jit(solution)/shard_map/step/pallas_call | solution.py:283
  53.1 0.0 copy-start.2
  53.1 0.8 copy-done.2
  53.9 0.0 copy-start.4
  53.9 0.8 copy-done.4
  54.7 17.4 %forces.3.part_ref = f32[8,16,128]{2,1,0:T(8,128)S(1)} custom-call(s32[256]{0:T(256)S(1)} %bitcast.7, s32[256]{0:T(256)S(1)} %bitcast.9, s32[1]{0:T(128)} %bitcast.5.count_ref, f32[8,16,128]{2,1,0:T(8,128)S(1)} %copy-done.2, f32[4,16,128]{2,1,0:T(8,128)S(1)} %copy-done.4), custom_call_target="tpu_custom_call" | custom-call | tf_op jit(solution)/shard_map/forces/pallas_call | solution.py:300
  72.1 0.0 copy-start.1
  72.1 0.6 copy-done.1
  72.7 0.0 copy-start.8
  72.7 13.2 %last.1 = (f32[3,512]{1,0:T(4,128)}, f32[3,512]{1,0:T(4,128)}) custom-call(f32[8,16,128]{2,1,0:T(8,128)} %copy-done.1, f32[3,512]{1,0:T(4,128)} %get-tuple-element.16.half_ref, s32[1,512]{1,0:T(1,128)} %bitcast.12), custom_call_target="tpu_custom_call" | custom-call | tf_op jit(solution)/shard_map/last/pallas_call | solution.py:301
  86.0 0.0 copy-done.8
  86.0 0.0 copy-start.10
  86.0 0.6 copy.13
  86.6 0.1 copy-done.10
  86.7 0.0 copy-start.9
  86.7 0.6 copy.14
  87.3 0.1 copy-done.9
  87.4 0.6 copy.15
Async XLA Ops:
  12.0 0.7 copy-start.7
  12.0 0.7 copy-start.6
  12.7 0.8 copy-start.3
  13.5 0.8 copy-start.5
  31.7 0.6 copy-start
  53.1 0.8 copy-start.2
  53.9 0.8 copy-start.4
  72.1 0.6 copy-start.1
  72.7 13.3 %copy-start.8 = (f32[3,512]{1,0:T(4,128)S(1)}, f32[3,512]{1,0:T(4,128)}, u32[]{:S(2)}) copy-start(f32[3,512]{1,0:T(4,128)} %get-tuple-element.22) | copy-start | bytes 18436
  86.0 0.7 copy-start.10
  86.7 0.7 copy-start.9

commit v2 on v1

--- a/solution.py
+++ b/solution.py
@@ -15,7 +15,7 @@
 HALF_STEP = 0.1
 TIME_STEP = 0.2
 tile_width = 128
-unroll = 4
+unroll = 32
 scale = 1.0 / math.log(2.0)
 middle = 2.0
 depth = 32
@@ -43,7 +43,7 @@
     return jnp.where(species == 1, HEAVY_CHARGE, LIGHT_CHARGE).astype(jnp.float32)
 
 
-def spread(axes, packed, slots, send_sem, recv_sem):
+def spread(axes, packed, slots, send_sem, recv_sem, own_sem):
     copies = []
     for (axis, size), buffer in zip(axes, slots):
         me = lax.axis_index(axis)
@@ -61,9 +61,13 @@
             )
     for copy in copies:
         copy.start()
-    for (axis, size), buffer in zip(axes, slots):
-        buffer[pl.ds(lax.axis_index(axis), 1)] = packed[...][None]
-    for copy in copies:
+    kept = [
+        pltpu.make_async_copy(packed, buffer.at[lax.axis_index(axis)], own_sem.at[index])
+        for index, ((axis, size), buffer) in enumerate(zip(axes, slots))
+    ]
+    for copy in kept:
+        copy.start()
+    for copy in kept + copies:
         copy.wait()
 
 
@@ -74,13 +78,13 @@
         packed[4 * tile + 3 : 4 * tile + 4, :] = charge[:, lanes]
 
 
-def gather_kernel(axes, tiles, pos_ref, spec_ref, rows_ref, cols_ref, packed, send_sem, recv_sem):
+def gather_kernel(axes, tiles, pos_ref, spec_ref, rows_ref, cols_ref, packed, send_sem, recv_sem, own_sem):
     greet(axes)
     pack(packed, pos_ref[...], charge_of(spec_ref[...]), tiles)
-    spread(axes, packed, (rows_ref, cols_ref), send_sem, recv_sem)
-
-
-def collect(axis, size, partial, arrived, send_sem, recv_sem):
+    spread(axes, packed, (rows_ref, cols_ref), send_sem, recv_sem, own_sem)
+
+
+def collect(axis, size, partial, arrived, send_sem, recv_sem, own_sem):
     me = lax.axis_index(axis)
     copies = []
     for step in range(1, size):
@@ -97,8 +101,9 @@
         )
     for copy in copies:
         copy.start()
-    arrived[pl.ds(me, 1)] = partial[pl.ds(me, 1)]
-    for copy in copies:
+    kept = pltpu.make_async_copy(partial.at[me], arrived.at[me], own_sem.at[0])
+    kept.start()
+    for copy in [kept] + copies:
         copy.wait()
     total = arrived[0]
     for index in range(1, size):
@@ -114,27 +119,31 @@
 
 def step_kernel(
     axes, tiles, part_ref, pos_ref, mom_ref, spec_ref, rows_ref, cols_ref, moved_ref, half_ref,
-    arrived, packed, send_a, recv_a, send_b, recv_b,
+    arrived, packed, send_a, recv_a, send_b, recv_b, own_sem,
 ):
     greet(axes)
     charge = charge_of(spec_ref[...])
-    total = collect(axes[0][0], axes[0][1], part_ref, arrived, send_a, recv_a)
+    total = collect(axes[0][0], axes[0][1], part_ref, arrived, send_a, recv_a, own_sem)
     force = unpacked(total, charge, tiles)
     half = mom_ref[...] + HALF_STEP * force
     moved = pos_ref[...] + TIME_STEP * half / charge
     half_ref[...] = half
     moved_ref[...] = moved
     pack(packed, moved, charge, tiles)
-    spread(axes, packed, (rows_ref, cols_ref), send_b, recv_b)
-
-
-def last_kernel(axes, tiles, part_ref, half_ref, spec_ref, ahead_ref, force_ref, arrived, send_a, recv_a):
+    spread(axes, packed, (rows_ref, cols_ref), send_b, recv_b, own_sem.at[pl.ds(1, 2)])
+
+
+def last_kernel(axes, tiles, part_ref, spec_ref, force_ref, arrived, send_a, recv_a, own_sem):
     greet(axes)
     charge = charge_of(spec_ref[...])
-    total = collect(axes[0][0], axes[0][1], part_ref, arrived, send_a, recv_a)
-    force = unpacked(total, charge, tiles)
-    force_ref[...] = force
-    ahead_ref[...] = half_ref[...] + HALF_STEP * force
+    total = collect(axes[0][0], axes[0][1], part_ref, arrived, send_a, recv_a, own_sem)
+    force_ref[...] = unpacked(total, charge, tiles)
+
+
+def finish_kernel(moved_ref, half_ref, force_ref, trial_ref, ahead_ref, end_ref):
+    trial_ref[...] = moved_ref[...]
+    ahead_ref[...] = half_ref[...] + HALF_STEP * force_ref[...]
+    end_ref[...] = force_ref[...]
 
 
 def pieces(value):
@@ -148,13 +157,21 @@
 
 
 def force_kernel(
-    tiles, first_ref, second_ref, count_ref, rows_ref, cols_ref, out_ref,
-    near_f, near, far_f, far, load_f, load, total,
+    tiles, first_ref, second_ref, count_ref, rows_hbm, cols_hbm, out_hbm,
+    out_ref, rows_ref, cols_ref, near_f, near, far_f, far, load_f, load, total, sems,
 ):
+    fetches = [
+        pltpu.make_async_copy(rows_hbm, rows_ref, sems.at[0]),
+        pltpu.make_async_copy(cols_hbm, cols_ref, sems.at[1]),
+    ]
+    for fetch in fetches:
+        fetch.start()
     near_f[...] = jnp.zeros_like(near_f)
     far_f[...] = jnp.zeros_like(far_f)
     load_f[...] = jnp.zeros_like(load_f)
     total[...] = jnp.zeros_like(total)
+    for fetch in fetches:
+        fetch.wait()
 
     def component(ref, owner, index):
         return ref[owner, pl.ds(index, tiles, stride=4), :]
@@ -228,6 +245,7 @@
             moment = total[here, axis, :] + total[here, 4 + axis, :] + total[here, 8 + axis, :]
             out_ref[owner, pl.ds(axis, tiles, stride=4), :] = charge * (value * weights - moment)
         out_ref[owner, pl.ds(3, tiles, stride=4), :] = jnp.zeros_like(charge)
+    pltpu.sync_copy(out_ref, out_hbm)
 
 
 def per_device(row_count, col_count, positions, momenta, species, tile_a, tile_b, tile_count):
@@ -237,6 +255,7 @@
     axes = (("col", col_count), ("row", row_count))
     others = row_count + col_count - 2
     vmem = pl.BlockSpec(memory_space=pltpu.VMEM)
+    anywhere = pl.BlockSpec(memory_space=pltpu.HBM)
     smem = pl.BlockSpec(memory_space=pltpu.SMEM)
     labels = species.reshape(1, own)
     slots = tile_a.shape[-1]
@@ -253,8 +272,10 @@
         functools.partial(gather_kernel, axes, tiles),
         out_shape=(row_shape, col_shape),
         in_specs=[vmem] * 2,
-        out_specs=(vmem, vmem),
-        scratch_shapes=[pltpu.VMEM((4 * tiles, tile_width), f32), DMA((others,)), DMA((others,))],
+        out_specs=(anywhere, anywhere),
+        scratch_shapes=[
+            pltpu.VMEM((4 * tiles, tile_width), f32), DMA((others,)), DMA((others,)), DMA((2,)),
+        ],
         compiler_params=pltpu.CompilerParams(collective_id=0, has_side_effects=True),
         name="gather",
     )(positions, labels)
@@ -264,9 +285,12 @@
     forces = pl.pallas_call(
         functools.partial(force_kernel, tiles),
         out_shape=row_shape,
-        in_specs=[smem] * 3 + [vmem] * 2,
-        out_specs=vmem,
+        in_specs=[smem] * 3 + [anywhere] * 2,
+        out_specs=anywhere,
         scratch_shapes=[
+            pltpu.VMEM(row_shape.shape, f32),
+            pltpu.VMEM(row_shape.shape, f32),
+            pltpu.VMEM(col_shape.shape, f32),
             pltpu.VMEM((near_count, depth, tile_width), f32),
             pltpu.VMEM((near_count, depth, tile_width), bf16),
             pltpu.VMEM((far_count, depth, tile_width), f32),
@@ -274,8 +298,8 @@
             pltpu.VMEM((far_count, 16, tile_width), f32),
             pltpu.VMEM((far_count, 16, 2 * tile_width), bf16),
             pltpu.VMEM((near_count, 16, tile_width), f32),
+            DMA((2,)),
         ],
-        compiler_params=pltpu.CompilerParams(vmem_limit_bytes=32 << 20),
         name="forces",
     )
 
@@ -283,8 +307,8 @@
     rows, cols, moved, half = pl.pallas_call(
         functools.partial(step_kernel, axes, tiles),
         out_shape=(row_shape, col_shape, own_shape, own_shape),
-        in_specs=[vmem] * 4,
-        out_specs=(vmem,) * 4,
+        in_specs=[anywhere] + [vmem] * 3,
+        out_specs=(anywhere, anywhere, vmem, vmem),
         scratch_shapes=[
             pltpu.VMEM(row_shape.shape, f32),
             pltpu.VMEM((4 * tiles, tile_width), f32),
@@ -292,22 +316,29 @@
             DMA((col_count - 1,)),
             DMA((others,)),
             DMA((others,)),
+            DMA((3,)),
         ],
         compiler_params=pltpu.CompilerParams(collective_id=1, has_side_effects=True),
         name="step",
     )(partial, positions, momenta, labels)
 
     partial = forces(firsts, seconds, count, rows, cols)
-    ahead, end_force = pl.pallas_call(
+    force = pl.pallas_call(
         functools.partial(last_kernel, axes[:1], tiles),
-        out_shape=(own_shape, own_shape),
-        in_specs=[vmem] * 3,
-        out_specs=(vmem,) * 2,
-        scratch_shapes=[pltpu.VMEM(row_shape.shape, f32), DMA((col_count - 1,)), DMA((col_count - 1,))],
+        out_shape=own_shape,
+        in_specs=[anywhere, vmem],
+        out_specs=vmem,
+        scratch_shapes=[
+            pltpu.VMEM(row_shape.shape, f32), DMA((col_count - 1,)), DMA((col_count - 1,)), DMA((1,)),
+        ],
         compiler_params=pltpu.CompilerParams(collective_id=2, has_side_effects=True),
         name="last",
-    )(partial, half, labels)
-    return (moved, ahead, end_force)
+    )(partial, labels)
+    return tuple(
+        pl.pallas_call(
+            finish_kernel, out_shape=(own_shape,) * 3, in_specs=[vmem] * 3, out_specs=(vmem,) * 3, name="finish"
+        )(moved, half, force)
+    )
 
 
 def solution(mesh):

time: 87.6 us -> 58.5 us (0.67)
  Pallas kernels: 79.5 us -> 56.9 us
  local copies, waits for them, and re-layouts: 7.09 us -> 0 us
    pallas_call x2, Pallas kernels: 34.8 us -> 24.3 us  [per_device(): partial = forces(firsts, seconds, count, rows, cols)]
    pallas_call x1, Pallas kernels: 20.8 us -> 13.1 us  [per_device(): pl.pallas_call(functools.partial(step_kernel, axes, tiles), out_shape=(ro...]
    unnamed x25 -> x0, local copies, waits for them, and re-layouts: 7.09 us -> none
    pallas_call x1, Pallas kernels: 13.2 us -> 8.02 us  [per_device(): pl.pallas_call(functools.partial(last_kernel, axes[:1], tiles), out_shape...]
    pallas_call x0 -> x1, Pallas kernels: none -> 1.34 us  [per_device(): pl.pallas_call(finish_kernel, out_shape=(own_shape,) * 3, in_specs=[vmem]...]
where the time goes in v2:
time: 58.5 us; the launch traced here: 58.2 us
  Pallas kernels  56.9 us (97%)
  between operations  1.32 us (2%)
    pallas_call x2, Pallas kernels, per_device(): partial = forces(firsts, seconds, count, rows, cols)  24.3 us
    pallas_call x1, Pallas kernels, per_device(): pl.pallas_call(functools.partial(step_kernel, axes, tiles), out_shape=(ro...  13.1 us
    pallas_call x1, Pallas kernels, per_device(): pl.pallas_call(functools.partial(gather_kernel, axes, tiles), out_shape=(...  10.2 us
    pallas_call x1, Pallas kernels, per_device(): pl.pallas_call(functools.partial(last_kernel, axes[:1], tiles), out_shape...  8.02 us
    pallas_call x1, Pallas kernels, per_device(): pl.pallas_call(finish_kernel, out_shape=(own_shape,) * 3, in_specs=[vmem]...  1.34 us

profile of v2, /device:TPU:0, one launch (start us, length us, event | category | flops | bytes accessed | tf_op | source)
XLA Modules:
  0.0 58.2 jit_solution(4997897336780665112)
XLA Ops:
  1.3 10.2 %gather.1 = (f32[8,16,128]{2,1,0:T(8,128)}, f32[4,16,128]{2,1,0:T(8,128)}) custom-call(f32[3,512]{1,0:T(4,128)} %pos_ref.3, s32[1,512]{1,0:T(1,128)} %bitcast.6), custom_call_target="tpu_custom_call" | custom-call | tf_op jit(solution)/shard_map/gather/pallas_call | solution.py:271
  11.5 12.2 %forces.2.part_ref = f32[8,16,128]{2,1,0:T(8,128)} custom-call(s32[256]{0:T(256)} %bitcast.9, s32[256]{0:T(256)} %bitcast.11, s32[1]{0:T(128)} %bitcast.4.count_ref, f32[8,16,128]{2,1,0:T(8,128)} %get-tuple-element.9.rows_hbm, f32[4,16,128]{2,1,0:T(8,128)} %get-tuple-element.10.cols_hbm), custom_call_target="tpu_custom_call" | custom-call | tf_op jit(solution)/shard_map/forces/pallas_call | solution.py:306
  23.6 13.1 %step.1 = (f32[8,16,128]{2,1,0:T(8,128)}, f32[4,16,128]{2,1,0:T(8,128)}, f32[3,512]{1,0:T(4,128)}, f32[3,512]{1,0:T(4,128)}) custom-call(f32[8,16,128]{2,1,0:T(8,128)} %forces.2.part_ref, f32[3,512]{1,0:T(4,128)} %pos_ref.3, f32[3,512]{1,0:T(4,128)} %mom_ref.1, s32[1,512]{1,0:T(1,128)} %bitcast.7), custom_call_target="tpu_custom_call" | custom-call | tf_op jit(solution)/shard_map/step/pallas_call | solution.py:307
  36.7 12.2 %forces.3.part_ref = f32[8,16,128]{2,1,0:T(8,128)} custom-call(s32[256]{0:T(256)} %bitcast.10, s32[256]{0:T(256)} %bitcast.12, s32[1]{0:T(128)} %bitcast.5.count_ref, f32[8,16,128]{2,1,0:T(8,128)} %get-tuple-element.13.rows_hbm, f32[4,16,128]{2,1,0:T(8,128)} %get-tuple-element.14.cols_hbm), custom_call_target="tpu_custom_call" | custom-call | tf_op jit(solution)/shard_map/forces/pallas_call | solution.py:325
  48.9 8.0 %last.1.force_ref = f32[3,512]{1,0:T(4,128)} custom-call(f32[8,16,128]{2,1,0:T(8,128)} %forces.3.part_ref, s32[1,512]{1,0:T(1,128)} %bitcast.8), custom_call_target="tpu_custom_call" | custom-call | tf_op jit(solution)/shard_map/last/pallas_call | solution.py:326
  56.9 1.3 %finish.1 = (f32[3,512]{1,0:T(4,128)}, f32[3,512]{1,0:T(4,128)}, f32[3,512]{1,0:T(4,128)}) custom-call(f32[3,512]{1,0:T(4,128)} %get-tuple-element.11.moved_ref, f32[3,512]{1,0:T(4,128)} %get-tuple-element.12.half_ref, f32[3,512]{1,0:T(4,128)} %last.1.force_ref), custom_call_target="tpu_custom_call" | custom-call | tf_op jit(solution)/shard_map/finish/pallas_call | solution.py:338

commit v3 on v2

--- a/solution.py
+++ b/solution.py
@@ -22,50 +22,63 @@
 MESH = pl.DeviceIdType.MESH
 
 
-def peers_of(axes):
-    found = []
-    for axis, size in axes:
-        me = lax.axis_index(axis)
-        for step in range(1, size):
-            found.append((axis, lax.rem(me + step, size)))
-    return found
-
-
-def greet(axes):
+def group_of(axes):
+    return 2 * lax.axis_index("row") // axes["row"]
+
+
+def across(axes):
+    return axes["row"] - 1 - lax.axis_index("row")
+
+
+def column_peers(axes):
+    me, size = lax.axis_index("col"), axes["col"]
+    return [{"col": lax.rem(me + step, size)} for step in range(1, size)]
+
+
+def cross_peers(axes):
+    me, size = lax.axis_index("col"), axes["col"]
+    return [{"row": across(axes), "col": lax.rem(me + step, size)} for step in range(size)]
+
+
+def row_peers(axes):
+    me, size = lax.axis_index("row"), axes["row"]
+    return [{"row": lax.rem(me + step, size)} for step in range(1, size)]
+
+
+def greet(everyone):
     barrier = pltpu.get_barrier_semaphore()
-    everyone = peers_of(axes)
-    for axis, peer in everyone:
-        pl.semaphore_signal(barrier, inc=1, device_id={axis: peer}, device_id_type=MESH)
+    for peer in everyone:
+        pl.semaphore_signal(barrier, inc=1, device_id=peer, device_id_type=MESH)
     pl.semaphore_wait(barrier, len(everyone))
+
+
+def remote(source, target, sems, which, peer):
+    return pltpu.make_async_remote_copy(
+        src_ref=source,
+        dst_ref=target,
+        send_sem=sems[0].at[which],
+        recv_sem=sems[1].at[which],
+        device_id=peer,
+        device_id_type=MESH,
+    )
 
 
 def charge_of(species):
     return jnp.where(species == 1, HEAVY_CHARGE, LIGHT_CHARGE).astype(jnp.float32)
 
 
-def spread(axes, packed, slots, send_sem, recv_sem, own_sem):
-    copies = []
-    for (axis, size), buffer in zip(axes, slots):
-        me = lax.axis_index(axis)
-        for step in range(1, size):
-            which = len(copies)
-            copies.append(
-                pltpu.make_async_remote_copy(
-                    src_ref=packed,
-                    dst_ref=buffer.at[me],
-                    send_sem=send_sem.at[which],
-                    recv_sem=recv_sem.at[which],
-                    device_id={axis: lax.rem(me + step, size)},
-                    device_id_type=MESH,
-                )
-            )
-    for copy in copies:
-        copy.start()
+def spread(axes, packed, rows_ref, cols_ref, sems, own_sem, extra=()):
+    mine = rows_ref.at[group_of(axes) * axes["col"] + lax.axis_index("col")]
+    level = cols_ref.at[lax.axis_index("row")]
+    jobs = [(packed, mine, peer) for peer in cross_peers(axes) + column_peers(axes)]
+    jobs += [(packed, level, peer) for peer in row_peers(axes)]
+    jobs += list(extra)
+    copies = [remote(source, target, sems, which, peer) for which, (source, target, peer) in enumerate(jobs)]
     kept = [
-        pltpu.make_async_copy(packed, buffer.at[lax.axis_index(axis)], own_sem.at[index])
-        for index, ((axis, size), buffer) in enumerate(zip(axes, slots))
+        pltpu.make_async_copy(packed, mine, own_sem.at[0]),
+        pltpu.make_async_copy(packed, level, own_sem.at[1]),
     ]
-    for copy in kept:
+    for copy in copies + kept:
         copy.start()
     for copy in kept + copies:
         copy.wait()
@@ -78,35 +91,39 @@
         packed[4 * tile + 3 : 4 * tile + 4, :] = charge[:, lanes]
 
 
-def gather_kernel(axes, tiles, pos_ref, spec_ref, rows_ref, cols_ref, packed, send_sem, recv_sem, own_sem):
-    greet(axes)
+def gather_kernel(
+    axes, tiles, pos_ref, spec_ref, first_ref, second_ref, count_ref, rows_ref, cols_ref, lists_ref,
+    packed, listed, send_sem, recv_sem, own_sem,
+):
+    greet(column_peers(axes) + cross_peers(axes) + row_peers(axes))
     pack(packed, pos_ref[...], charge_of(spec_ref[...]), tiles)
-    spread(axes, packed, (rows_ref, cols_ref), send_sem, recv_sem, own_sem)
-
-
-def collect(axis, size, partial, arrived, send_sem, recv_sem, own_sem):
-    me = lax.axis_index(axis)
-    copies = []
-    for step in range(1, size):
-        peer = lax.rem(me + step, size)
-        copies.append(
-            pltpu.make_async_remote_copy(
-                src_ref=partial.at[peer],
-                dst_ref=arrived.at[me],
-                send_sem=send_sem.at[step - 1],
-                recv_sem=recv_sem.at[step - 1],
-                device_id={axis: peer},
-                device_id_type=MESH,
-            )
-        )
+    listed[...] = jnp.zeros_like(listed)
+    listed[0:1, :] = first_ref[...]
+    listed[1:2, :] = second_ref[...]
+    listed[2:3, :] = jnp.broadcast_to(count_ref[...], first_ref.shape)
+    target = lists_ref.at[group_of(axes)]
+    kept = pltpu.make_async_copy(listed, target, own_sem.at[2])
+    kept.start()
+    extra = [(listed, target, {"row": across(axes)})]
+    spread(axes, packed, rows_ref, cols_ref, (send_sem, recv_sem), own_sem, extra)
+    kept.wait()
+
+
+def collect(axes, partial, arrived, sems, own_sem):
+    size, me, group = axes["col"], lax.axis_index("col"), group_of(axes)
+    mine = arrived.at[group * size + me]
+    jobs = [
+        (partial.at[(1 - group) * size + peer["col"]], mine, peer) for peer in cross_peers(axes)
+    ]
+    jobs += [(partial.at[group * size + peer["col"]], mine, peer) for peer in column_peers(axes)]
+    copies = [remote(source, target, sems, which, peer) for which, (source, target, peer) in enumerate(jobs)]
+    copies.append(pltpu.make_async_copy(partial.at[group * size + me], mine, own_sem))
     for copy in copies:
         copy.start()
-    kept = pltpu.make_async_copy(partial.at[me], arrived.at[me], own_sem.at[0])
-    kept.start()
-    for copy in [kept] + copies:
+    for copy in copies:
         copy.wait()
     total = arrived[0]
-    for index in range(1, size):
+    for index in range(1, 2 * size):
         total = total + arrived[index]
     return total
 
@@ -121,22 +138,22 @@
     axes, tiles, part_ref, pos_ref, mom_ref, spec_ref, rows_ref, cols_ref, moved_ref, half_ref,
     arrived, packed, send_a, recv_a, send_b, recv_b, own_sem,
 ):
-    greet(axes)
+    greet(column_peers(axes) + cross_peers(axes) + row_peers(axes))
     charge = charge_of(spec_ref[...])
-    total = collect(axes[0][0], axes[0][1], part_ref, arrived, send_a, recv_a, own_sem)
+    total = collect(axes, part_ref, arrived, (send_a, recv_a), own_sem.at[0])
     force = unpacked(total, charge, tiles)
     half = mom_ref[...] + HALF_STEP * force
     moved = pos_ref[...] + TIME_STEP * half / charge
     half_ref[...] = half
     moved_ref[...] = moved
     pack(packed, moved, charge, tiles)
-    spread(axes, packed, (rows_ref, cols_ref), send_b, recv_b, own_sem.at[pl.ds(1, 2)])
+    spread(axes, packed, rows_ref, cols_ref, (send_b, recv_b), own_sem.at[pl.ds(1, 2)])
 
 
 def last_kernel(axes, tiles, part_ref, spec_ref, force_ref, arrived, send_a, recv_a, own_sem):
-    greet(axes)
+    greet(column_peers(axes) + cross_peers(axes))
     charge = charge_of(spec_ref[...])
-    total = collect(axes[0][0], axes[0][1], part_ref, arrived, send_a, recv_a, own_sem)
+    total = collect(axes, part_ref, arrived, (send_a, recv_a), own_sem.at[0])
     force_ref[...] = unpacked(total, charge, tiles)
 
 
@@ -157,7 +174,7 @@
 
 
 def force_kernel(
-    tiles, first_ref, second_ref, count_ref, rows_hbm, cols_hbm, out_hbm,
+    axes, tiles, lists_ref, rows_hbm, cols_hbm, out_hbm,
     out_ref, rows_ref, cols_ref, near_f, near, far_f, far, load_f, load, total, sems,
 ):
     fetches = [
@@ -212,12 +229,23 @@
     load[:, :, :tile_width] = single
     load[:, :, tile_width:] = single
 
-    count = count_ref[0]
+    slots = lists_ref.shape[2]
+    group = group_of(axes)
+    lower = lists_ref[0, 2, 0]
+    count = lower + lists_ref[1, 2, 0]
+    middle_slot = (count + 1) // 2
+    begin = group * middle_slot
+    end = jnp.where(group == 0, middle_slot, count)
 
     def visit(step, carry):
-        start = step * unroll
-        firsts = [first_ref[start + index] for index in range(unroll)]
-        seconds = [second_ref[start + index] for index in range(unroll)]
+        start = begin + step * unroll
+        firsts, seconds = [], []
+        for index in range(unroll):
+            slot = jnp.minimum(start + index, count - 1)
+            side = (slot >= lower).astype(jnp.int32)
+            slot = slot - side * lower
+            firsts.append(lists_ref[side, 0, slot] + side * (near.shape[0] // 2))
+            seconds.append(lists_ref[side, 1, slot])
         terms = []
         for index in range(unroll):
             square = jnp.dot(far[seconds[index]], near[firsts[index]], preferred_element_type=jnp.float32)
@@ -229,12 +257,12 @@
             low = (weight - high.astype(jnp.float32)).astype(jnp.bfloat16)
             both = jnp.concatenate([high, low], axis=0)
             term = jnp.dot(load[seconds[index]], both, preferred_element_type=jnp.float32)
-            terms.append(jnp.where(start + index < count, term, 0.0))
+            terms.append(jnp.where(start + index < end, term, 0.0))
         for index in range(unroll):
             total[firsts[index]] += terms[index]
         return carry
 
-    lax.fori_loop(0, (count + unroll - 1) // unroll, visit, 0)
+    lax.fori_loop(0, (end - begin + unroll - 1) // unroll, visit, 0)
 
     for owner in range(rows_ref.shape[0]):
         here = pl.ds(owner * tiles, tiles)
@@ -252,40 +280,44 @@
     own = positions.shape[1]
     tiles = own // tile_width
     f32 = jnp.float32
-    axes = (("col", col_count), ("row", row_count))
-    others = row_count + col_count - 2
+    axes = {"col": col_count, "row": row_count}
+    across_all = 2 * col_count - 1
+    others = across_all + row_count - 1
     vmem = pl.BlockSpec(memory_space=pltpu.VMEM)
     anywhere = pl.BlockSpec(memory_space=pltpu.HBM)
     smem = pl.BlockSpec(memory_space=pltpu.SMEM)
     labels = species.reshape(1, own)
     slots = tile_a.shape[-1]
-    padding = -slots % unroll
-    firsts = jnp.pad(tile_a.reshape(slots), (0, padding))
-    seconds = jnp.pad(tile_b.reshape(slots), (0, padding))
-    count = tile_count.reshape(1)
-    row_shape = jax.ShapeDtypeStruct((col_count, 4 * tiles, tile_width), f32)
+    firsts = tile_a.reshape(1, slots)
+    seconds = tile_b.reshape(1, slots)
+    row_shape = jax.ShapeDtypeStruct((2 * col_count, 4 * tiles, tile_width), f32)
     col_shape = jax.ShapeDtypeStruct((row_count, 4 * tiles, tile_width), f32)
     own_shape = jax.ShapeDtypeStruct((3, own), f32)
     DMA = pltpu.SemaphoreType.DMA
 
-    rows, cols = pl.pallas_call(
+    list_shape = jax.ShapeDtypeStruct((2, 8, slots), jnp.int32)
+    rows, cols, lists = pl.pallas_call(
         functools.partial(gather_kernel, axes, tiles),
-        out_shape=(row_shape, col_shape),
-        in_specs=[vmem] * 2,
-        out_specs=(anywhere, anywhere),
+        out_shape=(row_shape, col_shape, list_shape),
+        in_specs=[vmem] * 5,
+        out_specs=(anywhere,) * 3,
         scratch_shapes=[
-            pltpu.VMEM((4 * tiles, tile_width), f32), DMA((others,)), DMA((others,)), DMA((2,)),
+            pltpu.VMEM((4 * tiles, tile_width), f32),
+            pltpu.VMEM((8, slots), jnp.int32),
+            DMA((others + 1,)),
+            DMA((others + 1,)),
+            DMA((3,)),
         ],
         compiler_params=pltpu.CompilerParams(collective_id=0, has_side_effects=True),
         name="gather",
-    )(positions, labels)
-
-    near_count, far_count = col_count * tiles, row_count * tiles
+    )(positions, labels, firsts, seconds, tile_count)
+
+    near_count, far_count = 2 * col_count * tiles, row_count * tiles
     bf16 = jnp.bfloat16
     forces = pl.pallas_call(
-        functools.partial(force_kernel, tiles),
+        functools.partial(force_kernel, axes, tiles),
         out_shape=row_shape,
-        in_specs=[smem] * 3 + [anywhere] * 2,
+        in_specs=[smem] + [anywhere] * 2,
         out_specs=anywhere,
         scratch_shapes=[
             pltpu.VMEM(row_shape.shape, f32),
@@ -303,7 +335,7 @@
         name="forces",
     )
 
-    partial = forces(firsts, seconds, count, rows, cols)
+    partial = forces(lists, rows, cols)
     rows, cols, moved, half = pl.pallas_call(
         functools.partial(step_kernel, axes, tiles),
         out_shape=(row_shape, col_shape, own_shape, own_shape),
@@ -312,8 +344,8 @@
         scratch_shapes=[
             pltpu.VMEM(row_shape.shape, f32),
             pltpu.VMEM((4 * tiles, tile_width), f32),
-            DMA((col_count - 1,)),
-            DMA((col_count - 1,)),
+            DMA((across_all,)),
+            DMA((across_all,)),
             DMA((others,)),
             DMA((others,)),
             DMA((3,)),
@@ -322,14 +354,14 @@
         name="step",
     )(partial, positions, momenta, labels)
 
-    partial = forces(firsts, seconds, count, rows, cols)
+    partial = forces(lists, rows, cols)
     force = pl.pallas_call(
-        functools.partial(last_kernel, axes[:1], tiles),
+        functools.partial(last_kernel, axes, tiles),
         out_shape=own_shape,
         in_specs=[anywhere, vmem],
         out_specs=vmem,
         scratch_shapes=[
-            pltpu.VMEM(row_shape.shape, f32), DMA((col_count - 1,)), DMA((col_count - 1,)), DMA((1,)),
+            pltpu.VMEM(row_shape.shape, f32), DMA((across_all,)), DMA((across_all,)), DMA((1,)),
         ],
         compiler_params=pltpu.CompilerParams(collective_id=2, has_side_effects=True),
         name="last",

time: 58.5 us -> 57.3 us (0.979)
  Pallas kernels: 56.9 us -> 55.2 us
    pallas_call x3, Pallas kernels: 32.3 us -> 24 us  [the longest x2 14 us: per_device(): partial = forces(lists, rows, cols)]
    pallas_call x1, Pallas kernels: 13.1 us -> 17.7 us  [per_device(): pl.pallas_call(functools.partial(step_kernel, axes, tiles), out_shape=(ro...]
    pallas_call x1, Pallas kernels: 10.2 us -> 12.1 us  [per_device(): pl.pallas_call(functools.partial(gather_kernel, axes, tiles), out_shape=(...]
where the time goes in v3:
time: 57.3 us; the launch traced here: 56.5 us
  Pallas kernels  55.2 us (96%)
  between operations  1.32 us (2%)
    pallas_call x1, Pallas kernels, per_device(): pl.pallas_call(functools.partial(step_kernel, axes, tiles), out_shape=(ro...  17.7 us
    pallas_call x2, Pallas kernels, per_device(): partial = forces(lists, rows, cols)  14 us
    pallas_call x1, Pallas kernels, per_device(): pl.pallas_call(functools.partial(gather_kernel, axes, tiles), out_shape=(...  12.1 us
    pallas_call x1, Pallas kernels, per_device(): pl.pallas_call(functools.partial(last_kernel, axes, tiles), out_shape=own...  10 us
    pallas_call x1, Pallas kernels, per_device(): pl.pallas_call(finish_kernel, out_shape=(own_shape,) * 3, in_specs=[vmem]...  1.34 us

profile of v3, /device:TPU:0, one launch (start us, length us, event | category | flops | bytes accessed | tf_op | source)
XLA Modules:
  0.0 56.5 jit_solution(4054476680164664736)
XLA Ops:
  1.3 12.1 %gather.1 = (f32[16,16,128]{2,1,0:T(8,128)}, f32[4,16,128]{2,1,0:T(8,128)}, s32[2,8,256]{2,1,0:T(8,128)}) custom-call(f32[3,512]{1,0:T(4,128)} %pos_ref.3, s32[1,512]{1,0:T(1,128)} %bitcast.3, s32[1,256]{1,0:T(1,128)} %bitcast.6, s32[1,256]{1,0:T(1,128)} %bitcast.7, s32[1,1]{1,0:T(1,128)S(6)} %copy.9.count_ref), custom_call_target="tpu_custom_call" | custom-call | tf_op jit(solution)/shard_map/gather/pallas_call | solution.py:299
  13.4 7.0 %forces.2.part_ref = f32[16,16,128]{2,1,0:T(8,128)} custom-call(s32[2,8,256]{2,1,0:T(8,128)} %get-tuple-element.10.lists_ref, f32[16,16,128]{2,1,0:T(8,128)} %get-tuple-element.11.rows_hbm, f32[4,16,128]{2,1,0:T(8,128)} %get-tuple-element.12.cols_hbm), custom_call_target="tpu_custom_call" | custom-call | tf_op jit(solution)/shard_map/forces/pallas_call | solution.py:338
  20.4 17.7 %step.1 = (f32[16,16,128]{2,1,0:T(8,128)}, f32[4,16,128]{2,1,0:T(8,128)}, f32[3,512]{1,0:T(4,128)}, f32[3,512]{1,0:T(4,128)}) custom-call(f32[16,16,128]{2,1,0:T(8,128)} %forces.2.part_ref, f32[3,512]{1,0:T(4,128)} %pos_ref.3, f32[3,512]{1,0:T(4,128)} %mom_ref.1, s32[1,512]{1,0:T(1,128)} %bitcast.4), custom_call_target="tpu_custom_call" | custom-call | tf_op jit(solution)/shard_map/step/pallas_call | solution.py:339
  38.1 7.0 %forces.3.part_ref = f32[16,16,128]{2,1,0:T(8,128)} custom-call(s32[2,8,256]{2,1,0:T(8,128)} %get-tuple-element.10.lists_ref, f32[16,16,128]{2,1,0:T(8,128)} %get-tuple-element.15.rows_hbm, f32[4,16,128]{2,1,0:T(8,128)} %get-tuple-element.16.cols_hbm), custom_call_target="tpu_custom_call" | custom-call | tf_op jit(solution)/shard_map/forces/pallas_call | solution.py:357
  45.1 10.0 %last.1.force_ref = f32[3,512]{1,0:T(4,128)} custom-call(f32[16,16,128]{2,1,0:T(8,128)} %forces.3.part_ref, s32[1,512]{1,0:T(1,128)} %bitcast.5), custom_call_target="tpu_custom_call" | custom-call | tf_op jit(solution)/shard_map/last/pallas_call | solution.py:358
  55.2 1.3 %finish.1 = (f32[3,512]{1,0:T(4,128)}, f32[3,512]{1,0:T(4,128)}, f32[3,512]{1,0:T(4,128)}) custom-call(f32[3,512]{1,0:T(4,128)} %get-tuple-element.13.moved_ref, f32[3,512]{1,0:T(4,128)} %get-tuple-element.14.half_ref, f32[3,512]{1,0:T(4,128)} %last.1.force_ref), custom_call_target="tpu_custom_call" | custom-call | tf_op jit(solution)/shard_map/finish/pallas_call | solution.py:370

commit v4 on v3

--- a/solution.py
+++ b/solution.py
@@ -15,7 +15,7 @@
 HALF_STEP = 0.1
 TIME_STEP = 0.2
 tile_width = 128
-unroll = 32
+unroll = 48
 scale = 1.0 / math.log(2.0)
 middle = 2.0
 depth = 32
@@ -45,10 +45,11 @@
     return [{"row": lax.rem(me + step, size)} for step in range(1, size)]
 
 
-def greet(everyone):
+def greet(everyone, meanwhile=lambda: None):
     barrier = pltpu.get_barrier_semaphore()
     for peer in everyone:
         pl.semaphore_signal(barrier, inc=1, device_id=peer, device_id_type=MESH)
+    meanwhile()
     pl.semaphore_wait(barrier, len(everyone))
 
 
@@ -95,12 +96,14 @@
     axes, tiles, pos_ref, spec_ref, first_ref, second_ref, count_ref, rows_ref, cols_ref, lists_ref,
     packed, listed, send_sem, recv_sem, own_sem,
 ):
-    greet(column_peers(axes) + cross_peers(axes) + row_peers(axes))
-    pack(packed, pos_ref[...], charge_of(spec_ref[...]), tiles)
-    listed[...] = jnp.zeros_like(listed)
-    listed[0:1, :] = first_ref[...]
-    listed[1:2, :] = second_ref[...]
-    listed[2:3, :] = jnp.broadcast_to(count_ref[...], first_ref.shape)
+    def prepare():
+        pack(packed, pos_ref[...], charge_of(spec_ref[...]), tiles)
+        listed[...] = jnp.zeros_like(listed)
+        listed[0:1, :] = first_ref[...]
+        listed[1:2, :] = second_ref[...]
+        listed[2:3, :] = jnp.broadcast_to(count_ref[...], first_ref.shape)
+
+    greet(column_peers(axes) + cross_peers(axes) + row_peers(axes), prepare)
     target = lists_ref.at[group_of(axes)]
     kept = pltpu.make_async_copy(listed, target, own_sem.at[2])
     kept.start()

time: 57.3 us -> 57.8 us (level)
  Pallas kernels: 55.2 us -> 56 us
    pallas_call x2, Pallas kernels: 14 us -> 16.8 us  [per_device(): partial = forces(lists, rows, cols)]
    pallas_call x1, Pallas kernels: 17.7 us -> 16.6 us  [per_device(): pl.pallas_call(functools.partial(step_kernel, axes, tiles), out_shape=(ro...]
    pallas_call x1, Pallas kernels: 10 us -> 9.31 us  [per_device(): pl.pallas_call(functools.partial(last_kernel, axes, tiles), out_shape=own...]
where the time goes in v4:
time: 57.8 us; the launch traced here: 57.3 us
  Pallas kernels  56 us (97%)
  between operations  1.32 us (2%)
    pallas_call x2, Pallas kernels, per_device(): partial = forces(lists, rows, cols)  16.8 us
    pallas_call x1, Pallas kernels, per_device(): pl.pallas_call(functools.partial(step_kernel, axes, tiles), out_shape=(ro...  16.6 us
    pallas_call x1, Pallas kernels, per_device(): pl.pallas_call(functools.partial(gather_kernel, axes, tiles), out_shape=(...  12 us
    pallas_call x1, Pallas kernels, per_device(): pl.pallas_call(functools.partial(last_kernel, axes, tiles), out_shape=own...  9.31 us
    pallas_call x1, Pallas kernels, per_device(): pl.pallas_call(finish_kernel, out_shape=(own_shape,) * 3, in_specs=[vmem]...  1.34 us

profile of v4, /device:TPU:0, one launch (start us, length us, event | category | flops | bytes accessed | tf_op | source)
XLA Modules:
  0.0 57.3 jit_solution(5003002190316531320)
XLA Ops:
  1.3 12.0 %gather.1 = (f32[16,16,128]{2,1,0:T(8,128)}, f32[4,16,128]{2,1,0:T(8,128)}, s32[2,8,256]{2,1,0:T(8,128)}) custom-call(f32[3,512]{1,0:T(4,128)} %pos_ref.3, s32[1,512]{1,0:T(1,128)} %bitcast.3, s32[1,256]{1,0:T(1,128)} %bitcast.6, s32[1,256]{1,0:T(1,128)} %bitcast.7, s32[1,1]{1,0:T(1,128)S(6)} %copy.9.count_ref), custom_call_target="tpu_custom_call" | custom-call | tf_op jit(solution)/shard_map/gather/pallas_call | solution.py:302
  13.3 8.4 %forces.2.part_ref = f32[16,16,128]{2,1,0:T(8,128)} custom-call(s32[2,8,256]{2,1,0:T(8,128)} %get-tuple-element.10.lists_ref, f32[16,16,128]{2,1,0:T(8,128)} %get-tuple-element.11.rows_hbm, f32[4,16,128]{2,1,0:T(8,128)} %get-tuple-element.12.cols_hbm), custom_call_target="tpu_custom_call" | custom-call | tf_op jit(solution)/shard_map/forces/pallas_call | solution.py:341
  21.7 16.6 %step.1 = (f32[16,16,128]{2,1,0:T(8,128)}, f32[4,16,128]{2,1,0:T(8,128)}, f32[3,512]{1,0:T(4,128)}, f32[3,512]{1,0:T(4,128)}) custom-call(f32[16,16,128]{2,1,0:T(8,128)} %forces.2.part_ref, f32[3,512]{1,0:T(4,128)} %pos_ref.3, f32[3,512]{1,0:T(4,128)} %mom_ref.1, s32[1,512]{1,0:T(1,128)} %bitcast.4), custom_call_target="tpu_custom_call" | custom-call | tf_op jit(solution)/shard_map/step/pallas_call | solution.py:342
  38.3 8.4 %forces.3.part_ref = f32[16,16,128]{2,1,0:T(8,128)} custom-call(s32[2,8,256]{2,1,0:T(8,128)} %get-tuple-element.10.lists_ref, f32[16,16,128]{2,1,0:T(8,128)} %get-tuple-element.15.rows_hbm, f32[4,16,128]{2,1,0:T(8,128)} %get-tuple-element.16.cols_hbm), custom_call_target="tpu_custom_call" | custom-call | tf_op jit(solution)/shard_map/forces/pallas_call | solution.py:360
  46.7 9.3 %last.1.force_ref = f32[3,512]{1,0:T(4,128)} custom-call(f32[16,16,128]{2,1,0:T(8,128)} %forces.3.part_ref, s32[1,512]{1,0:T(1,128)} %bitcast.5), custom_call_target="tpu_custom_call" | custom-call | tf_op jit(solution)/shard_map/last/pallas_call | solution.py:361
  56.0 1.3 %finish.1 = (f32[3,512]{1,0:T(4,128)}, f32[3,512]{1,0:T(4,128)}, f32[3,512]{1,0:T(4,128)}) custom-call(f32[3,512]{1,0:T(4,128)} %get-tuple-element.13.moved_ref, f32[3,512]{1,0:T(4,128)} %get-tuple-element.14.half_ref, f32[3,512]{1,0:T(4,128)} %last.1.force_ref), custom_call_target="tpu_custom_call" | custom-call | tf_op jit(solution)/shard_map/finish/pallas_call | solution.py:373

commit v5 on v4

--- a/solution.py
+++ b/solution.py
@@ -193,14 +193,20 @@
     for fetch in fetches:
         fetch.wait()
 
+    def flat(ref):
+        return ref.reshape(ref.shape[0] * ref.shape[1], ref.shape[2])
+
+    rows_flat, cols_flat, out_flat = flat(rows_ref), flat(cols_ref), flat(out_ref)
+
     def component(ref, owner, index):
-        return ref[owner, pl.ds(index, tiles, stride=4), :]
-
-    for owner in range(rows_ref.shape[0]):
-        here = pl.ds(owner * tiles, tiles)
+        return ref[pl.ds(4 * owner * batch + index, batch, stride=4), :]
+
+    batch = 2 * tiles
+    for owner in range(rows_ref.shape[0] // 2):
+        here = pl.ds(owner * batch, batch)
         square = 0.0
         for axis in range(3):
-            value = (component(rows_ref, owner, axis) - middle) * scale
+            value = (component(rows_flat, owner, axis) - middle) * scale
             square = square + value * value
             split = pieces(value)
             for row, (left, _) in enumerate(pairs_of_pieces):
@@ -210,12 +216,12 @@
             near_f[here, 21 + row, :] = jnp.ones_like(piece)
     near[...] = near_f[...].astype(jnp.bfloat16)
 
-    for owner in range(cols_ref.shape[0]):
-        here = pl.ds(owner * tiles, tiles)
-        charge = component(cols_ref, owner, 3)
+    for owner in range(cols_ref.shape[0] // 2):
+        here = pl.ds(owner * batch, batch)
+        charge = component(cols_flat, owner, 3)
         square = SOFTENING * scale * scale
         for axis in range(3):
-            value = (component(cols_ref, owner, axis) - middle) * scale
+            value = (component(cols_flat, owner, axis) - middle) * scale
             square = square + value * value
             split = pieces(value)
             for row, (_, right) in enumerate(pairs_of_pieces):
@@ -267,15 +273,15 @@
 
     lax.fori_loop(0, (end - begin + unroll - 1) // unroll, visit, 0)
 
-    for owner in range(rows_ref.shape[0]):
-        here = pl.ds(owner * tiles, tiles)
-        charge = component(rows_ref, owner, 3) * (scale * scale)
+    for owner in range(rows_ref.shape[0] // 2):
+        here = pl.ds(owner * batch, batch)
+        charge = component(rows_flat, owner, 3) * (scale * scale)
         weights = total[here, 3, :]
         for axis in range(3):
-            value = (component(rows_ref, owner, axis) - middle) * scale
+            value = (component(rows_flat, owner, axis) - middle) * scale
             moment = total[here, axis, :] + total[here, 4 + axis, :] + total[here, 8 + axis, :]
-            out_ref[owner, pl.ds(axis, tiles, stride=4), :] = charge * (value * weights - moment)
-        out_ref[owner, pl.ds(3, tiles, stride=4), :] = jnp.zeros_like(charge)
+            out_flat[pl.ds(4 * owner * batch + axis, batch, stride=4), :] = charge * (value * weights - moment)
+        out_flat[pl.ds(4 * owner * batch + 3, batch, stride=4), :] = jnp.zeros_like(charge)
     pltpu.sync_copy(out_ref, out_hbm)
 
 

time: 57.8 us -> 56.6 us (0.979)
  Pallas kernels: 56 us -> 55.2 us
    pallas_call x1, Pallas kernels: 16.6 us -> 15.8 us  [per_device(): pl.pallas_call(functools.partial(step_kernel, axes, tiles), out_shape=(ro...]
where the time goes in v5:
time: 56.6 us; the launch traced here: 56.5 us
  Pallas kernels  55.2 us (98%)
  between operations  1.32 us (2%)
    pallas_call x2, Pallas kernels, per_device(): partial = forces(lists, rows, cols)  16.7 us
    pallas_call x1, Pallas kernels, per_device(): pl.pallas_call(functools.partial(step_kernel, axes, tiles), out_shape=(ro...  15.8 us
    pallas_call x1, Pallas kernels, per_device(): pl.pallas_call(functools.partial(gather_kernel, axes, tiles), out_shape=(...  12 us
    pallas_call x1, Pallas kernels, per_device(): pl.pallas_call(functools.partial(last_kernel, axes, tiles), out_shape=own...  9.32 us
    pallas_call x1, Pallas kernels, per_device(): pl.pallas_call(finish_kernel, out_shape=(own_shape,) * 3, in_specs=[vmem]...  1.34 us

profile of v5, /device:TPU:0, one launch (start us, length us, event | category | flops | bytes accessed | tf_op | source)
XLA Modules:
  0.0 56.5 jit_solution(17004936384799559701)
XLA Ops:
  1.3 12.0 %gather.1 = (f32[16,16,128]{2,1,0:T(8,128)}, f32[4,16,128]{2,1,0:T(8,128)}, s32[2,8,256]{2,1,0:T(8,128)}) custom-call(f32[3,512]{1,0:T(4,128)} %pos_ref.3, s32[1,512]{1,0:T(1,128)} %bitcast.3, s32[1,256]{1,0:T(1,128)} %bitcast.6, s32[1,256]{1,0:T(1,128)} %bitcast.7, s32[1,1]{1,0:T(1,128)S(6)} %copy.9.count_ref), custom_call_target="tpu_custom_call" | custom-call | tf_op jit(solution)/shard_map/gather/pallas_call | solution.py:308
  13.3 8.3 %forces.2.part_ref = f32[16,16,128]{2,1,0:T(8,128)} custom-call(s32[2,8,256]{2,1,0:T(8,128)} %get-tuple-element.10.lists_ref, f32[16,16,128]{2,1,0:T(8,128)} %get-tuple-element.11.rows_hbm, f32[4,16,128]{2,1,0:T(8,128)} %get-tuple-element.12.cols_hbm), custom_call_target="tpu_custom_call" | custom-call | tf_op jit(solution)/shard_map/forces/pallas_call | solution.py:347
  21.6 15.8 %step.1 = (f32[16,16,128]{2,1,0:T(8,128)}, f32[4,16,128]{2,1,0:T(8,128)}, f32[3,512]{1,0:T(4,128)}, f32[3,512]{1,0:T(4,128)}) custom-call(f32[16,16,128]{2,1,0:T(8,128)} %forces.2.part_ref, f32[3,512]{1,0:T(4,128)} %pos_ref.3, f32[3,512]{1,0:T(4,128)} %mom_ref.1, s32[1,512]{1,0:T(1,128)} %bitcast.4), custom_call_target="tpu_custom_call" | custom-call | tf_op jit(solution)/shard_map/step/pallas_call | solution.py:348
  37.5 8.3 %forces.3.part_ref = f32[16,16,128]{2,1,0:T(8,128)} custom-call(s32[2,8,256]{2,1,0:T(8,128)} %get-tuple-element.10.lists_ref, f32[16,16,128]{2,1,0:T(8,128)} %get-tuple-element.15.rows_hbm, f32[4,16,128]{2,1,0:T(8,128)} %get-tuple-element.16.cols_hbm), custom_call_target="tpu_custom_call" | custom-call | tf_op jit(solution)/shard_map/forces/pallas_call | solution.py:366
  45.8 9.3 %last.1.force_ref = f32[3,512]{1,0:T(4,128)} custom-call(f32[16,16,128]{2,1,0:T(8,128)} %forces.3.part_ref, s32[1,512]{1,0:T(1,128)} %bitcast.5), custom_call_target="tpu_custom_call" | custom-call | tf_op jit(solution)/shard_map/last/pallas_call | solution.py:367
  55.1 1.3 %finish.1 = (f32[3,512]{1,0:T(4,128)}, f32[3,512]{1,0:T(4,128)}, f32[3,512]{1,0:T(4,128)}) custom-call(f32[3,512]{1,0:T(4,128)} %get-tuple-element.13.moved_ref, f32[3,512]{1,0:T(4,128)} %get-tuple-element.14.half_ref, f32[3,512]{1,0:T(4,128)} %last.1.force_ref), custom_call_target="tpu_custom_call" | custom-call | tf_op jit(solution)/shard_map/finish/pallas_call | solution.py:379
